TPU v7x, 32 devices: a whole 2x2x4 slice. The times are simulated.
32 devices in a mesh: seq: 2 (over x), shard: 16 (over z, y, core).
Axes of the slice: x: 2, y: 2, z: 4, core: 2. Of those that a mesh axis runs over, the one named last changes fastest.
Arguments:
- layer_input: bfloat16 [16, 256, 2048], P('shard', 'seq'), may hold values from -6 to 6
- seq_lengths: int32 [16, 3], P('shard'), may hold values from 1 to 192, 256 in all within a row
- seq_order: int32 [16, 3], P('shard'), may hold values from 0 to 2, each once within a row
- expert_ids: int32 [16, 256, 8], P('shard', 'seq'), may hold values from 0 to 15, all different within a row; in each aligned block of 128 rows (0 to 127, 128 to 255, ..., all dimensions but the last counted through in order) at most 96 rows name the same one
- expert_probs: float32 [16, 256, 8], P('shard', 'seq'), may hold values from 0.05 to 0.3
- weight_qkv: bfloat16 [2048, 6144], P('shard'), may hold values from -0.125 to 0.125
- weight_out: bfloat16 [2048, 2048], P('shard'), may hold values from -1.5 to 1.5
- norm_gains: bfloat16 [2048, 4], P('shard'), may hold values from 0.25 to 1.75
- weight_gate: bfloat16 [16, 2048, 1024], P('shard'), may hold values from -0.125 to 0.125
- weight_up: bfloat16 [16, 2048, 1024], P('shard'), may hold values from -0.125 to 0.125
- weight_down: bfloat16 [16, 1024, 2048], P('shard'), may hold values from -0.75 to 0.75
- out_cotangent: bfloat16 [16, 256, 2048], P('shard', 'seq'), may hold values from -6 to 6
Outputs:
- layer_output: bfloat16 [16, 256, 2048], P('shard', 'seq')
- input_grad: bfloat16 [16, 256, 2048], P('shard', 'seq')
- grad_qkv: float32 [2048, 6144], P('shard')
- grad_out: float32 [2048, 2048], P('shard')
- grad_gains: float32 [2048, 4], P('shard')
- grad_gate: float32 [16, 2048, 1024], P('shard', 'seq')
- grad_up: float32 [16, 2048, 1024], P('shard', 'seq')
- grad_down: float32 [16, 1024, 2048], P('shard', 'seq')
Inputs may be any that keep to these rules, and one draw needn't show every extreme that they name: `seq_lengths`: in each group the 3 lengths add up to 256, and the longest is exactly 192. `seq_order`: each group's row is a permutation of 0 to 2. `expert_ids`: each token names 8 different experts. Among the 128 tokens of one device (aligned blocks of 128 tokens in order of group and position) no expert is named more than 96 times, and in every draw some expert is named exactly 96 times within some block.
All inputs are finite; a program needn't handle non-finite values.
Results may differ from a plain program's by a relative error of at most 0.02.
Values may be sent and summed in bfloat16 or wider, within the bound.
A program may use at most 320 MiB of HBM per device.

v0:
```python
import jax
import jax.numpy as jnp
from jax import lax
from jax.sharding import PartitionSpec as P

HEADS = 16
HEAD_DIM = 128
norm_eps = 1e-05
rope_base = 10000.0


def rms_scale(values, gain_col):
    return (
        values * lax.rsqrt(jnp.mean(values * values, axis=-1, keepdims=True) + norm_eps) * gain_col
    )


def rotate(values, cosine, sine_part):
    half_dim = values.shape[-1] // 2
    first_half = values[..., :half_dim]
    second_half = values[..., half_dim:]
    return jnp.concatenate(
        [
            first_half * cosine - second_half * sine_part,
            second_half * cosine + first_half * sine_part,
        ],
        axis=-1,
    )


def rope_tables(position, head_size):
    half_dim = head_size // 2
    frequency = rope_base ** (-2.0 * jnp.arange(half_dim, dtype=jnp.float32) / head_size)
    angles = position.astype(jnp.float32)[:, None] * frequency[None, :]
    return (jnp.cos(angles)[:, None, :], jnp.sin(angles)[:, None, :])


def group_layout(lengths, seq_perm, group_tok):
    seq_count = lengths.shape[0]
    numbers = jnp.arange(seq_count, dtype=jnp.int32)
    packed = jnp.sum(jnp.where(seq_perm[:, None] == numbers[None, :], lengths[None, :], 0), axis=1)
    seq_ends = jnp.cumsum(packed)
    seq_starts = seq_ends - packed
    places = jnp.arange(group_tok, dtype=jnp.int32)
    segment = jnp.sum((places[:, None] >= seq_ends[None, :]).astype(jnp.int32), axis=1)
    begins = jnp.sum(
        jnp.where(segment[:, None] == numbers[None, :], seq_starts[None, :], 0), axis=1
    )
    return (segment, places - begins)


def slot_tables(expert_list, expert_count, capacity):
    rows_here, top_count = expert_list.shape
    flat_ids = expert_list.reshape(-1)
    onehot = (flat_ids[:, None] == jnp.arange(expert_count, dtype=jnp.int32)[None, :]).astype(
        jnp.int32
    )
    slot_rank = jnp.sum((jnp.cumsum(onehot, axis=0) - 1) * onehot, axis=1)
    slot_index = flat_ids * capacity + slot_rank
    owners = jnp.arange(rows_here * top_count, dtype=jnp.int32) // top_count
    sources = (
        jnp.full((expert_count * capacity,), rows_here, dtype=jnp.int32).at[slot_index].set(owners)
    )
    return (sources, slot_index)


def contract_rows(left_side, right_side):
    return lax.dot_general(
        left_side, right_side, (((0,), (0,)), ((), ())), preferred_element_type=jnp.float32
    )


def contract_cols(left_side, right_side):
    return lax.dot_general(
        left_side, right_side, (((1,), (1,)), ((), ())), preferred_element_type=jnp.float32
    )


def shards(
    layer_input,
    seq_lengths,
    seq_order,
    expert_ids,
    expert_probs,
    weight_qkv,
    weight_out,
    norm_gains,
    weight_gate,
    weight_up,
    weight_down,
    out_cotangent,
):
    model_width = layer_input.shape[-1]
    tok_rows = layer_input.shape[1]
    seq_groups = lax.axis_size("seq")
    group_tok = tok_rows * seq_groups
    expert_count = lax.axis_size("shard")
    top_count = expert_ids.shape[-1]
    capacity = min(tok_rows, 3 * tok_rows * top_count // (2 * expert_count))
    heads_local = HEADS // seq_groups
    local_width = heads_local * HEAD_DIM
    score_scale = HEAD_DIM ** (-0.5)
    segment, position = group_layout(seq_lengths[0], seq_order[0], group_tok)
    places = jnp.arange(group_tok, dtype=jnp.int32)
    allowed = (segment[:, None] == segment[None, :]) & (places[None, :] <= places[:, None])
    own_position = lax.dynamic_slice_in_dim(position, lax.axis_index("seq") * tok_rows, tok_rows)
    cosine, sine_part = rope_tables(own_position, HEAD_DIM)
    full_qkv, full_out, full_gains = (
        lax.all_gather(weight_qkv, "shard", axis=0, tiled=True),
        lax.all_gather(weight_out, "shard", axis=0, tiled=True),
        lax.all_gather(norm_gains, "shard", axis=0, tiled=True),
    )
    gain_cols = full_gains.astype(jnp.float32)

    def qk_piece(raw_part, gain_col):
        normed_part = rms_scale(raw_part, gain_col).reshape(tok_rows, HEADS, HEAD_DIM)
        return rotate(normed_part, cosine, sine_part).reshape(tok_rows, model_width)

    tokens_f32 = layer_input.reshape(tok_rows, model_width).astype(jnp.float32)
    attn_normed, attn_norm_back = jax.vjp(rms_scale, tokens_f32, gain_cols[:, 0])
    attn_in = attn_normed.astype(jnp.bfloat16)
    projected = jnp.dot(attn_in, full_qkv, preferred_element_type=jnp.float32)
    query_rot, query_back = jax.vjp(qk_piece, projected[:, :model_width], gain_cols[:, 1])
    key_rot, key_back = jax.vjp(
        qk_piece, projected[:, model_width : 2 * model_width], gain_cols[:, 2]
    )
    query_tok = query_rot.astype(jnp.bfloat16)
    key_tok = key_rot.astype(jnp.bfloat16)
    value_tok = projected[:, 2 * model_width :].astype(jnp.bfloat16)
    query_head, key_head, value_head = (
        lax.all_to_all(query_tok, "seq", split_axis=1, concat_axis=0, tiled=True),
        lax.all_to_all(key_tok, "seq", split_axis=1, concat_axis=0, tiled=True),
        lax.all_to_all(value_tok, "seq", split_axis=1, concat_axis=0, tiled=True),
    )
    query_head = query_head.reshape(group_tok, heads_local, HEAD_DIM)
    key_head = key_head.reshape(group_tok, heads_local, HEAD_DIM)
    value_head = value_head.reshape(group_tok, heads_local, HEAD_DIM)
    scores = (
        jnp.einsum("ihd,jhd->hij", query_head, key_head, preferred_element_type=jnp.float32)
        * score_scale
    )
    scores = jnp.where(allowed[None], scores, -1e30)
    score_peak = jnp.max(scores, axis=-1, keepdims=True)
    weights_exp = jnp.exp(scores - score_peak)
    row_total = jnp.sum(weights_exp, axis=-1, keepdims=True)
    attn_probs = weights_exp / row_total
    log_total = score_peak + jnp.log(row_total)
    mix_head = jnp.einsum(
        "hij,jhd->ihd",
        attn_probs.astype(jnp.bfloat16),
        value_head,
        preferred_element_type=jnp.float32,
    )
    mix_head = mix_head.astype(jnp.bfloat16).reshape(group_tok, local_width)
    attn_mix = lax.all_to_all(mix_head, "seq", split_axis=0, concat_axis=1, tiled=True)
    resid = tokens_f32 + jnp.dot(attn_mix, full_out, preferred_element_type=jnp.float32)
    ffn_normed, ffn_norm_back = jax.vjp(rms_scale, resid, gain_cols[:, 3])
    ffn_in = ffn_normed.astype(jnp.bfloat16)
    sources, slot_index = slot_tables(
        expert_ids.reshape(tok_rows, top_count), expert_count, capacity
    )
    pair_probs = expert_probs.reshape(tok_rows * top_count)
    slot_weight = jnp.zeros((expert_count * capacity,), jnp.float32).at[slot_index].set(pair_probs)
    padded = jnp.concatenate([ffn_in, jnp.zeros((1, model_width), jnp.bfloat16)], axis=0)
    outgoing = padded[sources].reshape(expert_count, capacity, model_width)
    gate_weight = weight_gate[0]
    up_weight = weight_up[0]
    down_weight = weight_down[0]
    arrived = lax.all_to_all(outgoing, "shard", split_axis=0, concat_axis=0, tiled=True)
    slot_count = arrived.shape[1]
    flat_rows = arrived.reshape(-1, model_width)
    gate_vals = jnp.dot(flat_rows, gate_weight, preferred_element_type=jnp.float32)
    up_vals = jnp.dot(flat_rows, up_weight, preferred_element_type=jnp.float32)
    hidden = (jax.nn.silu(gate_vals) * up_vals).astype(jnp.bfloat16)
    result = jnp.dot(hidden, down_weight, preferred_element_type=jnp.float32).astype(jnp.bfloat16)
    returned = lax.all_to_all(
        result.reshape(arrived.shape[0], slot_count, model_width),
        "shard",
        split_axis=0,
        concat_axis=0,
        tiled=True,
    )
    returned, arrived_kept, gate_kept, up_kept = (
        returned,
        arrived,
        gate_vals.reshape(arrived.shape[0], slot_count, -1),
        up_vals.reshape(arrived.shape[0], slot_count, -1),
    )
    picked = returned.reshape(expert_count * capacity, model_width)[slot_index].reshape(
        tok_rows, top_count, model_width
    )
    mixed_out = jnp.sum(
        picked.astype(jnp.float32) * expert_probs.reshape(tok_rows, top_count)[..., None], axis=1
    )
    layer_output = (resid + mixed_out).astype(jnp.bfloat16)
    grad_tokens = out_cotangent.reshape(tok_rows, model_width).astype(jnp.float32)
    padded_grad = jnp.concatenate([grad_tokens, jnp.zeros((1, model_width), jnp.float32)], axis=0)
    d_expert = (
        (padded_grad[sources] * slot_weight[:, None])
        .astype(jnp.bfloat16)
        .reshape(expert_count, capacity, model_width)
    )
    d_arrived = lax.all_to_all(d_expert, "shard", split_axis=0, concat_axis=0, tiled=True).reshape(
        -1, model_width
    )
    gate_vals = gate_kept.reshape(d_arrived.shape[0], -1)
    up_vals = up_kept.reshape(d_arrived.shape[0], -1)
    sigma_gate = jax.nn.sigmoid(gate_vals)
    silu_gate = gate_vals * sigma_gate
    hidden = (silu_gate * up_vals).astype(jnp.bfloat16)
    d_hidden = contract_cols(d_arrived, down_weight)
    d_gate = (d_hidden * up_vals * sigma_gate * (1.0 + gate_vals * (1.0 - sigma_gate))).astype(
        jnp.bfloat16
    )
    d_up = (d_hidden * silu_gate).astype(jnp.bfloat16)
    rows_in = arrived_kept.reshape(-1, model_width)
    part_down = contract_rows(hidden, d_arrived)
    part_gate = contract_rows(rows_in, d_gate)
    part_up = contract_rows(rows_in, d_up)
    d_pair = (contract_cols(d_gate, gate_weight) + contract_cols(d_up, up_weight)).astype(
        jnp.bfloat16
    )
    d_pair_back = lax.all_to_all(
        d_pair.reshape(expert_count, capacity, model_width),
        "shard",
        split_axis=0,
        concat_axis=0,
        tiled=True,
    )
    d_ffn_in = jnp.sum(
        d_pair_back.reshape(expert_count * capacity, model_width)[slot_index]
        .astype(jnp.float32)
        .reshape(tok_rows, top_count, model_width),
        axis=1,
    )
    sum_gate, sum_up, sum_down = (
        lax.psum_scatter(
            part_gate.astype(jnp.bfloat16), "seq", scatter_dimension=0, tiled=True
        ).astype(jnp.float32),
        lax.psum_scatter(
            part_up.astype(jnp.bfloat16), "seq", scatter_dimension=0, tiled=True
        ).astype(jnp.float32),
        lax.psum_scatter(
            part_down.astype(jnp.bfloat16), "seq", scatter_dimension=0, tiled=True
        ).astype(jnp.float32),
    )
    d_resid_norm, grad_g_ffn = ffn_norm_back(d_ffn_in)
    d_resid = grad_tokens + d_resid_norm
    d_branch = d_resid.astype(jnp.bfloat16)
    d_mix = contract_cols(d_branch, full_out).astype(jnp.bfloat16)
    d_mix_head = lax.all_to_all(d_mix, "seq", split_axis=1, concat_axis=0, tiled=True).reshape(
        group_tok, heads_local, HEAD_DIM
    )
    scores_again = (
        jnp.einsum("ihd,jhd->hij", query_head, key_head, preferred_element_type=jnp.float32)
        * score_scale
    )
    probs_back = jnp.where(allowed[None], jnp.exp(scores_again - log_total), 0.0)
    d_probs = jnp.einsum("ihd,jhd->hij", d_mix_head, value_head, preferred_element_type=jnp.float32)
    delta_rows = jnp.sum(probs_back * d_probs, axis=-1, keepdims=True)
    d_scores = (probs_back * (d_probs - delta_rows)).astype(jnp.bfloat16)
    d_query = (
        jnp.einsum("hij,jhd->ihd", d_scores, key_head, preferred_element_type=jnp.float32)
        * score_scale
    ).astype(jnp.bfloat16)
    d_key = (
        jnp.einsum("hij,ihd->jhd", d_scores, query_head, preferred_element_type=jnp.float32)
        * score_scale
    ).astype(jnp.bfloat16)
    d_value = jnp.einsum(
        "hij,ihd->jhd",
        probs_back.astype(jnp.bfloat16),
        d_mix_head,
        preferred_element_type=jnp.float32,
    ).astype(jnp.bfloat16)
    dq_tok, dk_tok, dv_tok = (
        lax.all_to_all(
            d_query.reshape(group_tok, local_width), "seq", split_axis=0, concat_axis=1, tiled=True
        ),
        lax.all_to_all(
            d_key.reshape(group_tok, local_width), "seq", split_axis=0, concat_axis=1, tiled=True
        ),
        lax.all_to_all(
            d_value.reshape(group_tok, local_width), "seq", split_axis=0, concat_axis=1, tiled=True
        ),
    )
    dq_raw, grad_g_q = query_back(dq_tok.astype(jnp.float32))
    dk_raw, grad_g_k = key_back(dk_tok.astype(jnp.float32))
    d_qkv = jnp.concatenate(
        [dq_raw.astype(jnp.bfloat16), dk_raw.astype(jnp.bfloat16), dv_tok], axis=1
    )
    d_attn_in = contract_cols(d_qkv, full_qkv)
    dx_norm, grad_g_attn = attn_norm_back(d_attn_in)
    input_grad = (d_resid + dx_norm).astype(jnp.bfloat16)
    gain_terms = jnp.stack([grad_g_attn, grad_g_q, grad_g_k, grad_g_ffn], axis=1)
    term_qkv = contract_rows(attn_in, d_qkv)
    term_out = contract_rows(attn_mix, d_branch)
    rows_qkv, rows_out, rows_gain = (
        lax.psum_scatter(
            term_qkv.astype(jnp.bfloat16), "shard", scatter_dimension=0, tiled=True
        ).astype(jnp.float32),
        lax.psum_scatter(
            term_out.astype(jnp.bfloat16), "shard", scatter_dimension=0, tiled=True
        ).astype(jnp.float32),
        lax.psum_scatter(
            gain_terms.astype(jnp.bfloat16), "shard", scatter_dimension=0, tiled=True
        ).astype(jnp.float32),
    )
    rows_qkv, rows_out, rows_gain = (
        lax.psum(rows_qkv.astype(jnp.bfloat16), "seq").astype(jnp.float32),
        lax.psum(rows_out.astype(jnp.bfloat16), "seq").astype(jnp.float32),
        lax.psum(rows_gain.astype(jnp.bfloat16), "seq").astype(jnp.float32),
    )
    return (
        layer_output.reshape(1, tok_rows, model_width),
        input_grad.reshape(1, tok_rows, model_width),
        rows_qkv,
        rows_out,
        rows_gain,
        sum_gate.reshape(1, sum_gate.shape[0], sum_gate.shape[1]),
        sum_up.reshape(1, sum_up.shape[0], sum_up.shape[1]),
        sum_down.reshape(1, sum_down.shape[0], sum_down.shape[1]),
    )


def solution(mesh):
    in_specs = (
        P("shard", "seq", None),
        P("shard", None),
        P("shard", None),
        P("shard", "seq", None),
        P("shard", "seq", None),
        P("shard", None),
        P("shard", None),
        P("shard", None),
        P("shard", None, None),
        P("shard", None, None),
        P("shard", None, None),
        P("shard", "seq", None),
    )
    out_specs = (
        P("shard", "seq", None),
        P("shard", "seq", None),
        P("shard", None),
        P("shard", None),
        P("shard", None),
        P("shard", "seq", None),
        P("shard", "seq", None),
        P("shard", "seq", None),
    )
    return jax.shard_map(shards, mesh=mesh, in_specs=in_specs, out_specs=out_specs, check_vma=False)
```

profile of v0, /device:TPU:0, one launch (start us, length us, event | category | flops | bytes accessed | tf_op | source)
XLA Modules:
  0.0 1513.0 jit_solution(13289953523183613215)
XLA Ops:
  11.6 4.5 reduce-window.18
  16.4 24.0 %all_gather.9 = bf16[2048,4]{0,1:T(4,128)(2,1)S(1)} all-gather(bf16[128,4]{0,1:T(4,128)(2,1)} %param.19), channel_id=1, replica_groups=mesh['seq'=2,'shard'=16] {'shard'}, dimensions={0}, use_global_device_ids=true | all-gather | bytes 17408 | tf_op jit(solution)/shard_map/all_gather | solution.py:111
  42.3 98.6 %all-gather.3.cloned.1.call-done = bf16[2048,6144]{1,0:T(8,128)(2,1)} async-done(((bf16[128,6144]{1,0:T(8,128)(2,1)}), bf16[2048,6144]{1,0:T(8,128)(2,1)}) %all-gather.3.cloned.1.call-update) | async-done | bytes 25165840 | tf_op jit(solution)/shard_map/all_gather | solution.py:109
  140.9 10.2 fusion.44
  152.3 4.2 all-to-all-start
  165.3 3.5 all-to-all-start.2
  169.6 6.9 all-to-all-done.2
  176.6 3.5 all-to-all-start.1
  180.1 4.3 scatter_custom_fusion
  192.2 16.1 %all-to-all-start.3 = ((bf16[2,128,1024]{1,2,0:T(8,128)(2,1)}), bf16[2,128,1024]{1,2,0:T(8,128)(2,1)S(1)}, u32[]{:S(2)}, u32[]{:S(2)}) async-start(bf16[2,128,1024]{1,2,0:T(8,128)(2,1)} %copy.136), calls=%async_computation.3 | async-start | bytes 1048576 | tf_op jit(solution)/shard_map/all_to_all | solution.py:155
  208.3 9.1 all-gather.5.cloned.1.call-done
  217.5 4.9 multiply_reduce_fusion.7
  223.6 7.1 gather_fusion
  230.7 4.8 all-to-all-start.4
  235.7 4.3 scatter_custom_fusion.1
  240.3 8.0 gather_fusion.2
  248.3 7.9 multiply_convert_fusion
  256.2 93.3 %all-to-all-done.4 = bf16[16,96,2048]{2,1,0:T(8,128)(2,1)} async-done(((bf16[16,96,2048]{2,1,0:T(8,128)(2,1)}), bf16[16,96,2048]{2,1,0:T(8,128)(2,1)}, u32[]{:S(2)}, u32[]{:S(2)}) %all-to-all-start.4) | async-done | bytes 6291488 | tf_op jit(solution)/shard_map/all_to_all | solution.py:169
  349.5 28.1 %all-to-all-start.6 = ((bf16[16,96,2048]{2,1,0:T(8,128)(2,1)}), bf16[16,96,2048]{2,1,0:T(8,128)(2,1)}, u32[]{:S(2)}, u32[]{:S(2)}) async-start(bf16[16,96,2048]{2,1,0:T(8,128)(2,1)} %multiply_convert_fusion), calls=%async_computation.6 | async-start | bytes 12582912 | tf_op jit(solution)/shard_map/all_to_all | solution.py:203
  377.6 11.8 fusion.6
  389.4 10.4 fusion.10
  399.8 91.8 %all-to-all-done.6 = bf16[16,96,2048]{2,1,0:T(8,128)(2,1)} async-done(((bf16[16,96,2048]{2,1,0:T(8,128)(2,1)}), bf16[16,96,2048]{2,1,0:T(8,128)(2,1)}, u32[]{:S(2)}, u32[]{:S(2)}) %all-to-all-start.6) | async-done | bytes 6291488 | tf_op jit(solution)/shard_map/all_to_all | solution.py:203
  491.7 17.7 %multiply_convert_fusion.1 = (bf16[1536,1024]{1,0:T(8,128)(2,1)}, bf16[1536,1024]{1,0:T(8,128)(2,1)}, bf16[1536,1024]{1,0:T(8,128)(2,1)S(1)}) fusion(f32[1536,1024]{1,0:T(8,128)} %fusion.10, f32[1536,1024]{1,0:T(8,128)} %fusion.6, bf16[1536,2048]{1,0:T(8,128)(2,1)} %bitcast.35, bf16[1,1024,2048]{2,1,0:T(8,128)(2,1)} %param.22), kind=kOutput, calls=%fused_computation.14 | convolution fusion | flops 6466043904 | bytes 32505856 | tf_op jit(solution)/shard_map/dot_general | solution.py:74
  509.4 8.7 convolution_convert_fusion.1
  518.1 28.1 %all-to-all-start.5 = ((bf16[16,96,2048]{2,1,0:T(8,128)(2,1)}), bf16[16,96,2048]{2,1,0:T(8,128)(2,1)}, u32[]{:S(2)}, u32[]{:S(2)}) async-start(bf16[16,96,2048]{2,1,0:T(8,128)(2,1)} %bitcast.177), calls=%async_computation.5 | async-start | bytes 12582912 | tf_op jit(solution)/shard_map/all_to_all | solution.py:176
  546.2 12.4 fusion.8
  558.7 11.5 add_convert_fusion
  570.2 90.1 %all-to-all-done.5 = bf16[16,96,2048]{2,1,0:T(8,128)(2,1)} async-done(((bf16[16,96,2048]{2,1,0:T(8,128)(2,1)}), bf16[16,96,2048]{2,1,0:T(8,128)(2,1)}, u32[]{:S(2)}, u32[]{:S(2)}) %all-to-all-start.5) | async-done | bytes 6291488 | tf_op jit(solution)/shard_map/all_to_all | solution.py:176
  660.3 28.1 %all-to-all-start.7 = ((bf16[16,96,2048]{2,1,0:T(8,128)(2,1)}), bf16[16,96,2048]{2,1,0:T(8,128)(2,1)}, u32[]{:S(2)}, u32[]{:S(2)}) async-start(bf16[16,96,2048]{2,1,0:T(8,128)(2,1)} %bitcast.176), calls=%async_computation.7 | async-start | bytes 12582912 | tf_op jit(solution)/shard_map/all_to_all | solution.py:223
  688.5 12.4 gather_fusion.1
  701.0 101.5 %all-to-all-done.7 = bf16[16,96,2048]{2,1,0:T(8,128)(2,1)} async-done(((bf16[16,96,2048]{2,1,0:T(8,128)(2,1)}), bf16[16,96,2048]{2,1,0:T(8,128)(2,1)}, u32[]{:S(2)}, u32[]{:S(2)}) %all-to-all-start.7) | async-done | bytes 6291488 | tf_op jit(solution)/shard_map/all_to_all | solution.py:223
  802.5 12.6 gather_fusion.3
  815.1 5.2 convert_reduce_fusion
  820.6 4.4 fusion
  826.2 5.6 convolution_convert_fusion.2
  831.8 6.5 convolution_convert_fusion.6
  839.2 3.5 all-to-all-start.8
  842.7 9.3 all-to-all-done.8
  855.1 4.2 all-to-all-start.11
  863.3 4.6 all-to-all-done.11
  867.9 3.5 all-to-all-start.9
  873.0 6.2 all-to-all-done.9
  879.1 3.5 all-to-all-start.10
  884.6 4.8 all-to-all-done.10
  891.8 2.8 copy.167
  894.6 2.3 pad_add_fusion
  896.9 2.5 copy.168
  899.5 2.3 multiply_reduce_fusion.3
  903.3 13.3 convolution_convert_fusion
  918.6 11.6 convolution_convert_fusion.4
  932.2 11.1 convolution_convert_fusion.5
  945.2 11.2 convolution_convert_fusion.3
  957.9 13.6 fusion.24
  972.8 233.2 %reduce-scatter.9.cloned.1.call-done = bf16[128,6144]{1,0:T(8,128)(2,1)} async-done(((bf16[2048,6144]{1,0:T(8,128)(2,1)}), bf16[128,6144]{1,0:T(8,128)(2,1)}) %reduce-scatter.9.cloned.1.call-update) | async-done | bytes 1572880 | tf_op jit(solution)/shard_map/reduce_scatter | solution.py:299
  1206.0 56.2 %reduce-scatter.15.cloned.1.call-done = bf16[1024,1024]{1,0:T(8,128)(2,1)} async-done(((bf16[2048,1024]{1,0:T(8,128)(2,1)}), bf16[1024,1024]{1,0:T(8,128)(2,1)}) %reduce-scatter.15.cloned.1.call-update) | async-done | bytes 2097168 | tf_op jit(solution)/shard_map/reduce_scatter | solution.py:240
  1262.2 4.1 bitcast_convert_fusion.1
  1266.3 53.1 %reduce-scatter.13.cloned.1.call-done = bf16[1024,1024]{1,0:T(8,128)(2,1)} async-done(((bf16[2048,1024]{1,0:T(8,128)(2,1)}), bf16[1024,1024]{1,0:T(8,128)(2,1)}) %reduce-scatter.13.cloned.1.call-update) | async-done | bytes 2097168 | tf_op jit(solution)/shard_map/reduce_scatter | solution.py:237
  1319.4 4.1 bitcast_convert_fusion.2
  1323.4 52.6 %reduce-scatter.17.cloned.1.call-done = bf16[512,2048]{1,0:T(8,128)(2,1)} async-done(((bf16[1024,2048]{1,0:T(8,128)(2,1)}), bf16[512,2048]{1,0:T(8,128)(2,1)}) %reduce-scatter.17.cloned.1.call-update) | async-done | bytes 2097168 | tf_op jit(solution)/shard_map/reduce_scatter | solution.py:243
  1376.1 4.1 bitcast_convert_fusion
  1381.3 55.0 %reduce-scatter.19.cloned.1.call-done = bf16[128,4]{1,0:T(8,128)(2,1)} async-done(((bf16[2048,4]{1,0:T(8,128)(2,1)}), bf16[128,4]{1,0:T(8,128)(2,1)}) %reduce-scatter.19.cloned.1.call-update) | async-done | bytes 1040
  1437.2 4.9 psum.23
  1442.7 58.0 %all-reduce.9.cloned.1.call-done = (bf16[128,6144]{1,0:T(8,128)(2,1)}, bf16[128,2048]{1,0:T(8,128)(2,1)}) async-done(((bf16[128,6144]{1,0:T(8,128)(2,1)}, bf16[128,2048]{1,0:T(8,128)(2,1)}), (bf16[128,6144]{1,0:T(8,128)(2,1)}, bf16[128,2048]{1,0:T(8,128)(2,1)})) %all-reduce.9.cloned.1.call-update) | async-done | bytes 2097168 | tf_op jit(solution)/shard_map/psum | solution.py:310
  1502.9 3.4 convert_element_type.227
  (259 shorter events, 56.3 us)
Async XLA Ops:
  7.2 133.8 %all-gather.3.cloned.1.call-start = ((), (), s32[]{:S(2)}) async-start(), calls=%async_computation.18 | async-start | bytes 26738688 | tf_op jit(solution)/shard_map/all_gather | solution.py:109
  7.9 209.6 %all-gather.5.cloned.1.call-start = ((), (), s32[]{:S(2)}) async-start(), calls=%async_computation.19 | async-start | bytes 8912896 | tf_op jit(solution)/shard_map/all_gather | solution.py:110
  42.0 98.9 %copy-start.59 = (f32[128]{0:T(128)}, f32[128]{0:T(128)S(1)}, u32[]{:S(2)}) copy-start(f32[128]{0:T(128)S(1)} %fusion.30) | copy-start | bytes 1540
  42.0 109.1 %copy-start.44 = (f32[128]{0:T(128)}, f32[128]{0:T(128)S(1)}, u32[]{:S(2)}) copy-start(f32[128]{0:T(128)S(1)} %fusion.56) | copy-start | bytes 1540
  42.3 119.8 %copy-start.30 = (f32[128,64]{0,1:T(8,128)}, f32[128,64]{0,1:T(8,128)S(1)}, u32[]{:S(2)}) copy-start(f32[128,64]{0,1:T(8,128)S(1)} %get-tuple-element.47) | copy-start | bytes 98308
  42.3 119.8 %copy-start.32 = (f32[128,64]{0,1:T(8,128)}, f32[128,64]{0,1:T(8,128)S(1)}, u32[]{:S(2)}) copy-start(f32[128,64]{0,1:T(8,128)S(1)} %get-tuple-element.48) | copy-start | bytes 98308
  42.3 108.9 %copy-start.28 = (f32[2048,1]{0,1:T(1,128)}, f32[2048,1]{0,1:T(1,128)S(1)}, u32[]{:S(2)}) copy-start(f32[2048,1]{0,1:T(1,128)S(1)} %get-tuple-element.46) | copy-start | bytes 24580
  42.3 114.9 %copy-start.34 = (f32[2048,1]{0,1:T(1,128)}, f32[2048,1]{0,1:T(1,128)S(1)}, u32[]{:S(2)}) copy-start(f32[2048,1]{0,1:T(1,128)S(1)} %get-tuple-element.44) | copy-start | bytes 24580
  42.3 114.9 %copy-start.36 = (f32[2048,1]{0,1:T(1,128)}, f32[2048,1]{0,1:T(1,128)S(1)}, u32[]{:S(2)}) copy-start(f32[2048,1]{0,1:T(1,128)S(1)} %get-tuple-element.45) | copy-start | bytes 24580
  42.3 180.1 %copy-start.38 = (f32[2048,1]{0,1:T(1,128)}, f32[2048,1]{0,1:T(1,128)S(1)}, u32[]{:S(2)}) copy-start(f32[2048,1]{0,1:T(1,128)S(1)} %get-tuple-element.43) | copy-start | bytes 24580
  151.2 7.6 copy-start
  152.3 13.0 all-to-all-start
  156.7 5.2 copy-start.55
  165.3 11.3 all-to-all-start.2
  176.6 10.5 all-to-all-start.1
  190.5 27.0 %copy-start.9 = (bf16[1,128,2048]{2,1,0:T(8,128)(2,1)S(1)}, bf16[1,128,2048]{2,1,0:T(8,128)(2,1)}, u32[]{:S(2)}) copy-start(bf16[1,128,2048]{2,1,0:T(8,128)(2,1)} %param.12) | copy-start | bytes 1572868
  192.2 25.3 %all-to-all-start.3 = ((bf16[2,128,1024]{1,2,0:T(8,128)(2,1)}), bf16[2,128,1024]{1,2,0:T(8,128)(2,1)S(1)}, u32[]{:S(2)}, u32[]{:S(2)}) async-start(bf16[2,128,1024]{1,2,0:T(8,128)(2,1)} %copy.136), calls=%async_computation.3 | async-start | bytes 1048576 | tf_op jit(solution)/shard_map/all_to_all | solution.py:155
  217.5 4.9 copy-start.11
  222.4 8.2 copy-start.57
  222.5 8.2 copy-start.47
  230.7 9.4 copy-start.22
  230.7 118.8 %all-to-all-start.4 = ((bf16[16,96,2048]{2,1,0:T(8,128)(2,1)}), bf16[16,96,2048]{2,1,0:T(8,128)(2,1)}, u32[]{:S(2)}, u32[]{:S(2)}) async-start(bf16[16,96,2048]{2,1,0:T(8,128)(2,1)} %bitcast.173), calls=%async_computation.4 | async-start | bytes 12582912 | tf_op jit(solution)/shard_map/all_to_all | solution.py:169
  349.5 142.2 %all-to-all-start.6 = ((bf16[16,96,2048]{2,1,0:T(8,128)(2,1)}), bf16[16,96,2048]{2,1,0:T(8,128)(2,1)}, u32[]{:S(2)}, u32[]{:S(2)}) async-start(bf16[16,96,2048]{2,1,0:T(8,128)(2,1)} %multiply_convert_fusion), calls=%async_computation.6 | async-start | bytes 12582912 | tf_op jit(solution)/shard_map/all_to_all | solution.py:203
  377.6 11.8 copy-start.62
  491.7 17.7 %copy-start.61 = (bf16[1,1024,2048]{2,1,0:T(8,128)(2,1)S(1)}, bf16[1,1024,2048]{2,1,0:T(8,128)(2,1)}, u32[]{:S(2)}) copy-start(bf16[1,1024,2048]{2,1,0:T(8,128)(2,1)} %param.22) | copy-start | bytes 12582916
  509.3 8.7 copy-start.64
  518.1 142.2 %all-to-all-start.5 = ((bf16[16,96,2048]{2,1,0:T(8,128)(2,1)}), bf16[16,96,2048]{2,1,0:T(8,128)(2,1)}, u32[]{:S(2)}, u32[]{:S(2)}) async-start(bf16[16,96,2048]{2,1,0:T(8,128)(2,1)} %bitcast.177), calls=%async_computation.5 | async-start | bytes 12582912 | tf_op jit(solution)/shard_map/all_to_all | solution.py:176
  546.2 12.5 copy-start.63
  546.2 12.5 copy-start.67
  660.3 142.2 %all-to-all-start.7 = ((bf16[16,96,2048]{2,1,0:T(8,128)(2,1)}), bf16[16,96,2048]{2,1,0:T(8,128)(2,1)}, u32[]{:S(2)}, u32[]{:S(2)}) async-start(bf16[16,96,2048]{2,1,0:T(8,128)(2,1)} %bitcast.176), calls=%async_computation.7 | async-start | bytes 12582912 | tf_op jit(solution)/shard_map/all_to_all | solution.py:223
  688.4 284.4 %reduce-scatter.11.cloned.1.call-start = ((), (), s32[]{:S(2)}) async-start(), calls=%async_computation.21 | async-start | bytes 8912896 | tf_op jit(solution)/shard_map/reduce_scatter | solution.py:302
  802.5 17.8 %copy-start.39 = (f32[2048,1]{0,1:T(1,128)S(1)}, f32[2048,1]{0,1:T(1,128)}, u32[]{:S(2)}) copy-start(f32[2048,1]{0,1:T(1,128)} %copy-done.38) | copy-start | bytes 24580
  802.5 17.9 %copy-start.48 = (f32[128]{0:T(128)S(1)}, f32[128]{0:T(128)}, u32[]{:S(2)}) copy-start(f32[128]{0:T(128)} %copy-done.47) | copy-start | bytes 1540
  815.0 5.3 copy-start.8
  815.1 5.5 copy-start.58
  815.1 5.5 copy-start.4
  820.6 5.6 copy-start.12
  826.2 5.6 copy-start.5
  831.8 10.8 copy-start.41
  831.8 10.8 copy-start.43
  838.3 15.0 copy-start.3
  838.3 14.9 copy-start.27
  839.2 12.9 all-to-all-start.8
  855.1 12.9 all-to-all-start.11
  862.0 9.5 copy-start.16
  867.9 11.2 all-to-all-start.9
  872.0 17.5 %copy-start.31 = (f32[128,64]{0,1:T(8,128)S(1)}, f32[128,64]{0,1:T(8,128)}, u32[]{:S(2)}) copy-start(f32[128,64]{0,1:T(8,128)} %copy-done.30) | copy-start | bytes 98308
  872.0 17.5 %copy-start.33 = (f32[128,64]{0,1:T(8,128)S(1)}, f32[128,64]{0,1:T(8,128)}, u32[]{:S(2)}) copy-start(f32[128,64]{0,1:T(8,128)} %copy-done.32) | copy-start | bytes 98308
  879.1 10.3 all-to-all-start.10
  882.6 323.4 %reduce-scatter.9.cloned.1.call-start = ((), (), s32[]{:S(2)}) async-start(), calls=%async_computation.20 | async-start | bytes 26738688 | tf_op jit(solution)/shard_map/reduce_scatter | solution.py:299
  890.7 8.7 copy-start.1
  890.7 8.7 copy-start.35
  890.7 8.7 copy-start.37
  890.7 8.7 copy-start.50
  890.7 8.7 copy-start.52
  894.6 7.2 copy-start.54
  894.6 7.2 copy-start.56
  916.7 345.6 %reduce-scatter.15.cloned.1.call-start = ((), (), s32[]{:S(2)}) async-start(), calls=%async_computation.23 | async-start | bytes 6291456 | tf_op jit(solution)/shard_map/reduce_scatter | solution.py:240
  930.2 389.2 %reduce-scatter.13.cloned.1.call-start = ((), (), s32[]{:S(2)}) async-start(), calls=%async_computation.22 | async-start | bytes 6291456 | tf_op jit(solution)/shard_map/reduce_scatter | solution.py:237
  943.3 432.8 %reduce-scatter.17.cloned.1.call-start = ((), (), s32[]{:S(2)}) async-start(), calls=%async_computation.24 | async-start | bytes 6291456 | tf_op jit(solution)/shard_map/reduce_scatter | solution.py:243
  956.4 480.0 %reduce-scatter.19.cloned.1.call-start = ((), (), s32[]{:S(2)}) async-start(), calls=%async_computation.25 | async-start | bytes 557056
  972.7 528.1 %all-reduce.9.cloned.1.call-start = ((), (), s32[]{:S(2)}) async-start(), calls=%async_computation.26 | async-start | bytes 4194304 | tf_op jit(solution)/shard_map/psum | solution.py:310
  1323.4 56.8 %copy-start.60 = (f32[128]{0:T(128)S(1)}, f32[128]{0:T(128)}, u32[]{:S(2)}) copy-start(f32[128]{0:T(128)} %copy-done.59) | copy-start | bytes 1540
  1323.4 56.8 %copy-start.6 = (f32[128,2048]{1,0:T(8,128)S(1)}, f32[128,2048]{1,0:T(8,128)}, u32[]{:S(2)}) copy-start(f32[128,2048]{1,0:T(8,128)} %copy-done.5) | copy-start | bytes 3145732
  (26 other events, 63.7 us)
Sparse Core Ops, SparseCore 0:
  9.6 131.3 all-gather.2
  143.1 74.3 all-gather.4
  831.9 126.8 reduce-scatter.10
  962.8 243.1 reduce-scatter.8
  1208.7 53.4 reduce-scatter.14
  1264.9 54.3 reduce-scatter.12
  1321.7 54.3 reduce-scatter.16
  1380.2 56.1 reduce-scatter.18
  1438.7 62.0 all-reduce.8
where the time goes:
time: 1520 us; the launch traced here: 1510 us
  waiting for transfers between devices  1030 us (68%)
  matrix products  165 us (11%)
  starting transfers between devices  132 us (9%)
  local copies, waits for them, and re-layouts  83.7 us (6%)
  other arithmetic  60.1 us (4%)
  blocking collectives  28.9 us (2%)
    reduce_scatter x1, waiting for transfers between devices, shards(): lax.psum_scatter(term_qkv.astype(jnp.bfloat16), 'shard', scatter_dimensio...  233 us
    all_to_all x1, waiting for transfers between devices, shards(): lax.all_to_all(d_pair.reshape(expert_count, capacity, model_width), 'shar...  102 us
    all_gather x1, waiting for transfers between devices, shards(): lax.all_gather(weight_qkv, 'shard', axis=0, tiled=True)  98.6 us
    all_to_all x1, waiting for transfers between devices, shards(): lax.all_to_all(outgoing, 'shard', split_axis=0, concat_axis=0, tiled=True)  93.3 us
    all_to_all x1, waiting for transfers between devices, shards(): lax.all_to_all(d_expert, 'shard', split_axis=0, concat_axis=0, tiled=True)  91.8 us
    all_to_all x1, waiting for transfers between devices, shards(): lax.all_to_all(result.reshape(arrived.shape[0], slot_count, model_width),...  90.1 us
    dot_general x5, matrix products, contract_cols(): lax.dot_general(left_side, right_side, (((1,), (1,)), ((), ())), preferre...  61.7 us
    psum x1, waiting for transfers between devices, shards(): lax.psum(rows_qkv.astype(jnp.bfloat16), 'seq').astype(jnp.float32)  58 us
  transfers between devices with their start and end apart: 21, of which 19 were waited for; matrix products, arithmetic and copies ran while one was open for 15% of the time, Pallas kernels for 0%

commit v1 on v0

--- a/solution.py
+++ b/solution.py
@@ -7,6 +7,28 @@
 HEAD_DIM = 128
 norm_eps = 1e-05
 rope_base = 10000.0
+
+
+def joined_along(parts, dim):
+    parts = jnp.moveaxis(parts, 0, dim)
+    dims = parts.shape
+    return parts.reshape(*dims[:dim], dims[dim] * dims[dim + 1], *dims[dim + 2 :])
+
+
+def collect(shard, axis, dim):
+    size = lax.axis_size(axis)
+    pairs = [(i, (i + 1) % size) for i in range(size)]
+    back = [(b, a) for a, b in pairs]
+    lower, upper = ([], [])
+    for step in range(size - 1):
+        if step % 2 == 0:
+            lower.append(lax.ppermute(lower[-1] if lower else shard, axis, pairs))
+        else:
+            upper.append(lax.ppermute(upper[-1] if upper else shard, axis, back))
+    parts = jnp.stack([*lower[::-1], shard, *upper])
+    shift = lax.axis_index(axis) - len(lower)
+    parts = parts[(jnp.arange(size) - shift) % size]
+    return joined_along(parts, dim)
 
 
 def rms_scale(values, gain_col):
@@ -106,7 +128,7 @@
     own_position = lax.dynamic_slice_in_dim(position, lax.axis_index("seq") * tok_rows, tok_rows)
     cosine, sine_part = rope_tables(own_position, HEAD_DIM)
     full_qkv, full_out, full_gains = (
-        lax.all_gather(weight_qkv, "shard", axis=0, tiled=True),
+        collect(weight_qkv, "shard", 0),
         lax.all_gather(weight_out, "shard", axis=0, tiled=True),
         lax.all_gather(norm_gains, "shard", axis=0, tiled=True),
     )

time: 1520 us -> 1750 us (1.15)
  starting transfers between devices: 132 us -> 292 us
  local copies, waits for them, and re-layouts: 83.7 us -> 137 us
    ppermute x0 -> x15, starting transfers between devices: none -> 141 us  [the longest x8 132 us: collect(): lower.append(lax.ppermute(lower[-1] if lower else shard, axis, pairs))]
    ppermute x0 -> x15, waiting for transfers between devices: none -> 100 us  [the longest x8 61.7 us: collect(): lower.append(lax.ppermute(lower[-1] if lower else shard, axis, pairs))]
    all_gather x1 -> x0, waiting for transfers between devices: 98.6 us -> none  [shards(): lax.all_gather(weight_qkv, 'shard', axis=0, tiled=True)]
    all_to_all x1, starting transfers between devices: 4.8 us -> 34.5 us  [shards(): lax.all_to_all(outgoing, 'shard', split_axis=0, concat_axis=0, tiled=True)]
    unnamed x144 -> x187, local copies, waits for them, and re-layouts: 15 us -> 39.9 us
    gather x0 -> x1, local copies, waits for them, and re-layouts: none -> 18.3 us  [collect(): parts = parts[(jnp.arange(size) - shift) % size]]
    unnamed x10 -> x9, waiting for transfers between devices: 56.5 us -> 55.2 us
  transfers between devices with their start and end apart: 21 -> 35, of which waited for: 19 -> 24; matrix products, arithmetic and copies ran while one was open for 15% -> 16% of each run, Pallas kernels for 0% -> 0%
where the time goes in v1:
time: 1750 us; the launch traced here: 1740 us
  waiting for transfers between devices  1020 us (58%)
  starting transfers between devices  292 us (17%)
  matrix products  171 us (10%)
  local copies, waits for them, and re-layouts  137 us (8%)
  other arithmetic  64.7 us (4%)
  blocking collectives  37.1 us (2%)
    reduce_scatter x1, waiting for transfers between devices, shards(): lax.psum_scatter(term_qkv.astype(jnp.bfloat16), 'shard', scatter_dimensio...  232 us
    ppermute x8, starting transfers between devices, collect(): lower.append(lax.ppermute(lower[-1] if lower else shard, axis, pairs))  132 us
    all_to_all x1, waiting for transfers between devices, shards(): lax.all_to_all(d_pair.reshape(expert_count, capacity, model_width), 'shar...  103 us
    all_to_all x1, waiting for transfers between devices, shards(): lax.all_to_all(result.reshape(arrived.shape[0], slot_count, model_width),...  95.6 us
    all_to_all x1, waiting for transfers between devices, shards(): lax.all_to_all(outgoing, 'shard', split_axis=0, concat_axis=0, tiled=True)  93.2 us
    all_to_all x1, waiting for transfers between devices, shards(): lax.all_to_all(d_expert, 'shard', split_axis=0, concat_axis=0, tiled=True)  91.8 us
    dot_general x5, matrix products, contract_cols(): lax.dot_general(left_side, right_side, (((1,), (1,)), ((), ())), preferre...  61.7 us
    ppermute x8, waiting for transfers between devices, collect(): lower.append(lax.ppermute(lower[-1] if lower else shard, axis, pairs))  61.7 us
  transfers between devices with their start and end apart: 35, of which 24 were waited for; matrix products, arithmetic and copies ran while one was open for 16% of the time, Pallas kernels for 0%

profile of v1, /device:TPU:0, one launch (start us, length us, event | category | flops | bytes accessed | tf_op | source)
XLA Modules:
  0.0 1742.4 jit_solution(14698339994489559250)
XLA Ops:
  7.8 23.3 %collective-permute-done = bf16[128,6144]{1,0:T(8,128)(2,1)S(1)} collective-permute-done((bf16[128,6144]{1,0:T(8,128)(2,1)}, bf16[128,6144]{1,0:T(8,128)(2,1)S(1)}, u32[]{:S(2)}, u32[]{:S(2)}) %collective-permute-start) | collective-permute-done | bytes 1572896 | tf_op jit(solution)/shard_map/ppermute | solution.py:25
  31.1 4.4 collective-permute-start.8
  35.5 18.2 %collective-permute-done.1 = bf16[128,6144]{1,0:T(8,128)(2,1)S(1)} collective-permute-done((bf16[128,6144]{1,0:T(8,128)(2,1)S(1)}, bf16[128,6144]{1,0:T(8,128)(2,1)S(1)}, u32[]{:S(2)}, u32[]{:S(2)}) %collective-permute-start.1) | collective-permute-done | bytes 1572896 | tf_op jit(solution)/shard_map/ppermute | solution.py:25
  53.7 10.9 collective-permute-start.2
  64.7 11.7 collective-permute-done.2
  76.3 24.2 %collective-permute-start.3 = (bf16[128,6144]{1,0:T(8,128)(2,1)S(1)}, bf16[128,6144]{1,0:T(8,128)(2,1)S(1)}, u32[]{:S(2)}, u32[]{:S(2)}) collective-permute-start(bf16[128,6144]{1,0:T(8,128)(2,1)S(1)} %collective-permute-done.2), channel_id=1, source_target_pairs={{0,1},{1,2},{2,3},{3,4},{4,5},{5,6},{6,7},{7,8},{8,9},{9,10},{10,1... | collective-permute-start | bytes 4718600 | tf_op jit(solution)/shard_map/ppermute | solution.py:25
  105.2 31.4 %collective-permute-start.4 = (bf16[128,6144]{1,0:T(8,128)(2,1)S(1)}, bf16[128,6144]{1,0:T(8,128)(2,1)S(1)}, u32[]{:S(2)}, u32[]{:S(2)}) collective-permute-start(bf16[128,6144]{1,0:T(8,128)(2,1)S(1)} %collective-permute-done.3), channel_id=1, source_target_pairs={{0,1},{1,2},{2,3},{3,4},{4,5},{5,6},{6,7},{7,8},{8,9},{9,10},{10,1... | collective-permute-start | bytes 4718600 | tf_op jit(solution)/shard_map/ppermute | solution.py:25
  139.7 32.8 %collective-permute-start.5 = (bf16[128,6144]{1,0:T(8,128)(2,1)S(1)}, bf16[128,6144]{1,0:T(8,128)(2,1)}, u32[]{:S(2)}, u32[]{:S(2)}) collective-permute-start(bf16[128,6144]{1,0:T(8,128)(2,1)S(1)} %collective-permute-done.4), channel_id=1, source_target_pairs={{0,1},{1,2},{2,3},{3,4},{4,5},{5,6},{6,7},{7,8},{8,9},{9,10},{10,1... | collective-permute-start | bytes 4718600 | tf_op jit(solution)/shard_map/ppermute | solution.py:25
  175.7 31.6 %collective-permute-start.6 = (bf16[128,6144]{1,0:T(8,128)(2,1)}, bf16[128,6144]{1,0:T(8,128)(2,1)}, u32[]{:S(2)}, u32[]{:S(2)}) collective-permute-start(bf16[128,6144]{1,0:T(8,128)(2,1)} %collective-permute-done.5), channel_id=1, source_target_pairs={{0,1},{1,2},{2,3},{3,4},{4,5},{5,6},{6,7},{7,8},{8,9},{9,10},{10,1... | collective-permute-start | bytes 4718600 | tf_op jit(solution)/shard_map/ppermute | solution.py:25
  209.4 4.5 reduce-window.18
  214.2 32.2 %all_gather.6 = bf16[2048,4]{0,1:T(4,128)(2,1)S(1)} all-gather(bf16[128,4]{0,1:T(4,128)(2,1)} %param.19), channel_id=1, replica_groups=mesh['seq'=2,'shard'=16] {'shard'}, dimensions={0}, use_global_device_ids=true | all-gather | bytes 17408 | tf_op jit(solution)/shard_map/all_gather | solution.py:133
  248.9 32.8 %collective-permute-done.13 = bf16[128,6144]{1,0:T(8,128)(2,1)S(1)} collective-permute-done((bf16[128,6144]{1,0:T(8,128)(2,1)}, bf16[128,6144]{1,0:T(8,128)(2,1)S(1)}, u32[]{:S(2)}, u32[]{:S(2)}) %collective-permute-start.13) | collective-permute-done | bytes 1572896 | tf_op jit(solution)/shard_map/ppermute | solution.py:27
  281.7 4.5 collective-permute-start.14
  311.3 5.5 collective-permute-done.14
  318.1 18.3 %gather_fusion = bf16[16,128,6144]{2,1,0:T(8,128)(2,1)} fusion(bf16[16,128,6144]{2,1,0:T(8,128)(2,1)} %bitcast_dynamic-update-slice_fusion, s32[1024]{0:T(1024)S(1)} %pad_clamp_fusion.1), kind=kCustom, calls=%fused_computation | custom fusion | bytes 50331712 | tf_op jit(solution)/shard_map/gather | solution.py:30
  336.4 10.3 fusion.47
  357.7 4.2 all-to-all-start.2
  363.7 4.9 all-to-all-done.2
  368.6 4.2 all-to-all-start.1
  374.0 5.5 all-to-all-done.1
  383.0 4.5 scatter_custom_fusion
  399.4 6.5 all-to-all-done.3
  405.9 4.9 multiply_reduce_fusion.7
  412.0 7.1 gather_fusion.1
  419.1 34.5 %all-to-all-start.4 = ((bf16[16,96,2048]{2,1,0:T(8,128)(2,1)}), bf16[16,96,2048]{2,1,0:T(8,128)(2,1)}, u32[]{:S(2)}, u32[]{:S(2)}) async-start(bf16[16,96,2048]{2,1,0:T(8,128)(2,1)} %bitcast.234), calls=%async_computation.4 | async-start | bytes 12582912 | tf_op jit(solution)/shard_map/all_to_all | solution.py:191
  453.8 8.1 gather_fusion.3
  462.1 4.3 scatter_custom_fusion.1
  466.5 8.0 multiply_convert_fusion
  474.4 93.2 %all-to-all-done.4 = bf16[16,96,2048]{2,1,0:T(8,128)(2,1)} async-done(((bf16[16,96,2048]{2,1,0:T(8,128)(2,1)}), bf16[16,96,2048]{2,1,0:T(8,128)(2,1)}, u32[]{:S(2)}, u32[]{:S(2)}) %all-to-all-start.4) | async-done | bytes 6291488 | tf_op jit(solution)/shard_map/all_to_all | solution.py:191
  567.7 28.3 %all-to-all-start.6 = ((bf16[16,96,2048]{2,1,0:T(8,128)(2,1)}), bf16[16,96,2048]{2,1,0:T(8,128)(2,1)}, u32[]{:S(2)}, u32[]{:S(2)}) async-start(bf16[16,96,2048]{2,1,0:T(8,128)(2,1)} %multiply_convert_fusion), calls=%async_computation.6 | async-start | bytes 12582912 | tf_op jit(solution)/shard_map/all_to_all | solution.py:225
  596.0 11.8 fusion.10
  607.8 10.4 fusion.6
  618.2 91.8 %all-to-all-done.6 = bf16[16,96,2048]{2,1,0:T(8,128)(2,1)} async-done(((bf16[16,96,2048]{2,1,0:T(8,128)(2,1)}), bf16[16,96,2048]{2,1,0:T(8,128)(2,1)}, u32[]{:S(2)}, u32[]{:S(2)}) %all-to-all-start.6) | async-done | bytes 6291488 | tf_op jit(solution)/shard_map/all_to_all | solution.py:225
  710.0 18.2 %multiply_convert_fusion.1 = (bf16[1536,1024]{1,0:T(8,128)(2,1)}, bf16[1536,1024]{1,0:T(8,128)(2,1)}, bf16[1536,1024]{1,0:T(8,128)(2,1)}) fusion(f32[1536,1024]{1,0:T(8,128)} %fusion.10, f32[1536,1024]{1,0:T(8,128)} %fusion.6, bf16[1536,2048]{1,0:T(8,128)(2,1)} %bitcast.53, bf16[1,1024,2048]{2,1,0:T(8,128)(2,1)} %param.22), kind=kOutput, calls=%fused_computation.15 | convolution fusion | flops 6466043904 | bytes 32505856 | tf_op jit(solution)/shard_map/dot_general | solution.py:96
  728.2 12.2 fusion.8
  740.4 11.7 add_convert_fusion
  752.1 28.1 %all-to-all-start.7 = ((bf16[16,96,2048]{2,1,0:T(8,128)(2,1)}), bf16[16,96,2048]{2,1,0:T(8,128)(2,1)}, u32[]{:S(2)}, u32[]{:S(2)}) async-start(bf16[16,96,2048]{2,1,0:T(8,128)(2,1)} %bitcast.238), calls=%async_computation.7 | async-start | bytes 12582912 | tf_op jit(solution)/shard_map/all_to_all | solution.py:245
  780.2 11.2 convolution_convert_fusion.1
  791.4 102.9 %all-to-all-done.7 = bf16[16,96,2048]{2,1,0:T(8,128)(2,1)} async-done(((bf16[16,96,2048]{2,1,0:T(8,128)(2,1)}), bf16[16,96,2048]{2,1,0:T(8,128)(2,1)}, u32[]{:S(2)}, u32[]{:S(2)}) %all-to-all-start.7) | async-done | bytes 6291488 | tf_op jit(solution)/shard_map/all_to_all | solution.py:245
  894.3 28.1 %all-to-all-start.5 = ((bf16[16,96,2048]{2,1,0:T(8,128)(2,1)}), bf16[16,96,2048]{2,1,0:T(8,128)(2,1)}, u32[]{:S(2)}, u32[]{:S(2)}) async-start(bf16[16,96,2048]{2,1,0:T(8,128)(2,1)} %bitcast.237), calls=%async_computation.5 | async-start | bytes 12582912 | tf_op jit(solution)/shard_map/all_to_all | solution.py:198
  922.6 12.9 gather_fusion.4
  935.4 5.1 convert_reduce_fusion
  940.8 95.6 %all-to-all-done.5 = bf16[16,96,2048]{2,1,0:T(8,128)(2,1)} async-done(((bf16[16,96,2048]{2,1,0:T(8,128)(2,1)}), bf16[16,96,2048]{2,1,0:T(8,128)(2,1)}, u32[]{:S(2)}, u32[]{:S(2)}) %all-to-all-start.5) | async-done | bytes 6291488 | tf_op jit(solution)/shard_map/all_to_all | solution.py:198
  1036.5 12.6 gather_fusion.2
  1049.0 6.6 fusion
  1056.9 5.6 convolution_convert_fusion.2
  1062.5 6.3 convolution_convert_fusion.6
  1073.2 9.3 all-to-all-done.8
  1090.8 4.2 all-to-all-start.10
  1099.2 4.4 all-to-all-done.10
  1115.0 4.2 all-to-all-start.11
  1134.9 13.4 convolution_convert_fusion
  1150.4 11.2 convolution_convert_fusion.4
  1163.5 11.1 convolution_convert_fusion.5
  1176.5 11.2 convolution_convert_fusion.3
  1189.3 13.4 fusion.28
  1204.0 232.0 %reduce-scatter.9.cloned.1.call-done = bf16[128,6144]{1,0:T(8,128)(2,1)} async-done(((bf16[2048,6144]{1,0:T(8,128)(2,1)}), bf16[128,6144]{1,0:T(8,128)(2,1)}) %reduce-scatter.9.cloned.1.call-update) | async-done | bytes 1572880 | tf_op jit(solution)/shard_map/reduce_scatter | solution.py:321
  1435.9 56.2 %reduce-scatter.15.cloned.1.call-done = bf16[1024,1024]{1,0:T(8,128)(2,1)} async-done(((bf16[2048,1024]{1,0:T(8,128)(2,1)}), bf16[1024,1024]{1,0:T(8,128)(2,1)}) %reduce-scatter.15.cloned.1.call-update) | async-done | bytes 2097168 | tf_op jit(solution)/shard_map/reduce_scatter | solution.py:262
  1496.2 53.1 %reduce-scatter.13.cloned.1.call-done = bf16[1024,1024]{1,0:T(8,128)(2,1)} async-done(((bf16[2048,1024]{1,0:T(8,128)(2,1)}), bf16[1024,1024]{1,0:T(8,128)(2,1)}) %reduce-scatter.13.cloned.1.call-update) | async-done | bytes 2097168 | tf_op jit(solution)/shard_map/reduce_scatter | solution.py:259
  1553.3 52.5 %reduce-scatter.17.cloned.1.call-done = bf16[512,2048]{1,0:T(8,128)(2,1)} async-done(((bf16[1024,2048]{1,0:T(8,128)(2,1)}), bf16[512,2048]{1,0:T(8,128)(2,1)}) %reduce-scatter.17.cloned.1.call-update) | async-done | bytes 2097168 | tf_op jit(solution)/shard_map/reduce_scatter | solution.py:265
  1605.8 4.1 bitcast_convert_fusion
  1611.1 55.1 %reduce-scatter.19.cloned.1.call-done = bf16[128,4]{1,0:T(8,128)(2,1)} async-done(((bf16[2048,4]{1,0:T(8,128)(2,1)}), bf16[128,4]{1,0:T(8,128)(2,1)}) %reduce-scatter.19.cloned.1.call-update) | async-done | bytes 1040
  1667.0 4.9 psum.23
  1672.5 58.0 %all-reduce.9.cloned.1.call-done = (bf16[128,6144]{1,0:T(8,128)(2,1)}, bf16[128,2048]{1,0:T(8,128)(2,1)}) async-done(((bf16[128,6144]{1,0:T(8,128)(2,1)}, bf16[128,2048]{1,0:T(8,128)(2,1)}), (bf16[128,6144]{1,0:T(8,128)(2,1)}, bf16[128,2048]{1,0:T(8,128)(2,1)})) %all-reduce.9.cloned.1.call-update) | async-done | bytes 2097168 | tf_op jit(solution)/shard_map/psum | solution.py:332
  (333 shorter events, 142.3 us)
Async XLA Ops:
  7.2 398.7 %all-gather.2.cloned.1.call-start = ((), (), s32[]{:S(2)}) async-start(), calls=%async_computation.18 | async-start | bytes 8912896 | tf_op jit(solution)/shard_map/all_gather | solution.py:132
  7.2 23.8 %collective-permute-start = (bf16[128,6144]{1,0:T(8,128)(2,1)}, bf16[128,6144]{1,0:T(8,128)(2,1)S(1)}, u32[]{:S(2)}, u32[]{:S(2)}) collective-permute-start(bf16[128,6144]{1,0:T(8,128)(2,1)} %param.17), channel_id=1, source_target_pairs={{0,1},{1,2},{2,3},{3,4},{4,5},{5,6},{6,7},{7,8},{8,9},{9,10},{10,1... | collective-permute-start | bytes 4718600 | tf_op jit(solution)/shard_map/ppermute | solution.py:25
  31.1 22.6 %collective-permute-start.1 = (bf16[128,6144]{1,0:T(8,128)(2,1)S(1)}, bf16[128,6144]{1,0:T(8,128)(2,1)S(1)}, u32[]{:S(2)}, u32[]{:S(2)}) collective-permute-start(bf16[128,6144]{1,0:T(8,128)(2,1)S(1)} %collective-permute-done), channel_id=1, source_target_pairs={{0,1},{1,2},{2,3},{3,4},{4,5},{5,6},{6,7},{7,8},{8,9},{9,10},{10,1... | collective-permute-start | bytes 4718600 | tf_op jit(solution)/shard_map/ppermute | solution.py:25
  31.1 33.6 %collective-permute-start.8 = (bf16[128,6144]{1,0:T(8,128)(2,1)}, bf16[128,6144]{1,0:T(8,128)(2,1)S(1)}, u32[]{:S(2)}, u32[]{:S(2)}) collective-permute-start(bf16[128,6144]{1,0:T(8,128)(2,1)} %param.17), channel_id=1, source_target_pairs={{1,0},{2,1},{3,2},{4,3},{5,4},{6,5},{7,6},{8,7},{9,8},{10,9},{11,1... | collective-permute-start | bytes 4718600 | tf_op jit(solution)/shard_map/ppermute | solution.py:27
  53.7 46.9 %copy-start.27 = (bf16[128,6144]{1,0:T(8,128)(2,1)}, bf16[128,6144]{1,0:T(8,128)(2,1)S(1)}, u32[]{:S(2)}) copy-start(bf16[128,6144]{1,0:T(8,128)(2,1)S(1)} %collective-permute-done.1) | copy-start | bytes 4718596
  53.7 22.6 %collective-permute-start.2 = (bf16[128,6144]{1,0:T(8,128)(2,1)S(1)}, bf16[128,6144]{1,0:T(8,128)(2,1)S(1)}, u32[]{:S(2)}, u32[]{:S(2)}) collective-permute-start(bf16[128,6144]{1,0:T(8,128)(2,1)S(1)} %collective-permute-done.1), channel_id=1, source_target_pairs={{0,1},{1,2},{2,3},{3,4},{4,5},{5,6},{6,7},{7,8},{8,9},{9,10},{10,1... | collective-permute-start | bytes 4718600 | tf_op jit(solution)/shard_map/ppermute | solution.py:25
  64.6 35.9 %collective-permute-start.9 = (bf16[128,6144]{1,0:T(8,128)(2,1)S(1)}, bf16[128,6144]{1,0:T(8,128)(2,1)S(1)}, u32[]{:S(2)}, u32[]{:S(2)}) collective-permute-start(bf16[128,6144]{1,0:T(8,128)(2,1)S(1)} %collective-permute-done.8), channel_id=1, source_target_pairs={{1,0},{2,1},{3,2},{4,3},{5,4},{6,5},{7,6},{8,7},{9,8},{10,9},{11,1... | collective-permute-start | bytes 4718600 | tf_op jit(solution)/shard_map/ppermute | solution.py:27
  76.3 60.2 %copy-start.31 = (bf16[128,6144]{1,0:T(8,128)(2,1)}, bf16[128,6144]{1,0:T(8,128)(2,1)S(1)}, u32[]{:S(2)}) copy-start(bf16[128,6144]{1,0:T(8,128)(2,1)S(1)} %collective-permute-done.2) | copy-start | bytes 4718596
  76.3 28.8 %collective-permute-start.3 = (bf16[128,6144]{1,0:T(8,128)(2,1)S(1)}, bf16[128,6144]{1,0:T(8,128)(2,1)S(1)}, u32[]{:S(2)}, u32[]{:S(2)}) collective-permute-start(bf16[128,6144]{1,0:T(8,128)(2,1)S(1)} %collective-permute-done.2), channel_id=1, source_target_pairs={{0,1},{1,2},{2,3},{3,4},{4,5},{5,6},{6,7},{7,8},{8,9},{9,10},{10,1... | collective-permute-start | bytes 4718600 | tf_op jit(solution)/shard_map/ppermute | solution.py:25
  100.6 36.0 %collective-permute-start.10 = (bf16[128,6144]{1,0:T(8,128)(2,1)S(1)}, bf16[128,6144]{1,0:T(8,128)(2,1)S(1)}, u32[]{:S(2)}, u32[]{:S(2)}) collective-permute-start(bf16[128,6144]{1,0:T(8,128)(2,1)S(1)} %collective-permute-done.9), channel_id=1, source_target_pairs={{1,0},{2,1},{3,2},{4,3},{5,4},{6,5},{7,6},{8,7},{9,8},{10,9},{11,1... | collective-permute-start | bytes 4718600 | tf_op jit(solution)/shard_map/ppermute | solution.py:27
  105.2 67.4 %copy-start.35 = (bf16[128,6144]{1,0:T(8,128)(2,1)}, bf16[128,6144]{1,0:T(8,128)(2,1)S(1)}, u32[]{:S(2)}) copy-start(bf16[128,6144]{1,0:T(8,128)(2,1)S(1)} %collective-permute-done.3) | copy-start | bytes 4718596
  105.2 34.6 %collective-permute-start.4 = (bf16[128,6144]{1,0:T(8,128)(2,1)S(1)}, bf16[128,6144]{1,0:T(8,128)(2,1)S(1)}, u32[]{:S(2)}, u32[]{:S(2)}) collective-permute-start(bf16[128,6144]{1,0:T(8,128)(2,1)S(1)} %collective-permute-done.3), channel_id=1, source_target_pairs={{0,1},{1,2},{2,3},{3,4},{4,5},{5,6},{6,7},{7,8},{8,9},{9,10},{10,1... | collective-permute-start | bytes 4718600 | tf_op jit(solution)/shard_map/ppermute | solution.py:25
  136.6 36.0 %collective-permute-start.11 = (bf16[128,6144]{1,0:T(8,128)(2,1)S(1)}, bf16[128,6144]{1,0:T(8,128)(2,1)}, u32[]{:S(2)}, u32[]{:S(2)}) collective-permute-start(bf16[128,6144]{1,0:T(8,128)(2,1)S(1)} %collective-permute-done.10), channel_id=1, source_target_pairs={{1,0},{2,1},{3,2},{4,3},{5,4},{6,5},{7,6},{8,7},{9,8},{10,9},{11,1... | collective-permute-start | bytes 4718600 | tf_op jit(solution)/shard_map/ppermute | solution.py:27
  139.7 32.8 %copy-start.37 = (bf16[128,6144]{1,0:T(8,128)(2,1)}, bf16[128,6144]{1,0:T(8,128)(2,1)S(1)}, u32[]{:S(2)}) copy-start(bf16[128,6144]{1,0:T(8,128)(2,1)S(1)} %collective-permute-done.4) | copy-start | bytes 4718596
  139.7 36.0 %collective-permute-start.5 = (bf16[128,6144]{1,0:T(8,128)(2,1)S(1)}, bf16[128,6144]{1,0:T(8,128)(2,1)}, u32[]{:S(2)}, u32[]{:S(2)}) collective-permute-start(bf16[128,6144]{1,0:T(8,128)(2,1)S(1)} %collective-permute-done.4), channel_id=1, source_target_pairs={{0,1},{1,2},{2,3},{3,4},{4,5},{5,6},{6,7},{7,8},{8,9},{9,10},{10,1... | collective-permute-start | bytes 4718600 | tf_op jit(solution)/shard_map/ppermute | solution.py:25
  172.5 74.0 %collective-permute-start.12 = (bf16[128,6144]{1,0:T(8,128)(2,1)}, bf16[128,6144]{1,0:T(8,128)(2,1)}, u32[]{:S(2)}, u32[]{:S(2)}) collective-permute-start(bf16[128,6144]{1,0:T(8,128)(2,1)} %collective-permute-done.11), channel_id=1, source_target_pairs={{1,0},{2,1},{3,2},{4,3},{5,4},{6,5},{7,6},{8,7},{9,8},{10,9},{11,1... | collective-permute-start | bytes 4718600 | tf_op jit(solution)/shard_map/ppermute | solution.py:27
  175.7 71.0 %collective-permute-start.6 = (bf16[128,6144]{1,0:T(8,128)(2,1)}, bf16[128,6144]{1,0:T(8,128)(2,1)}, u32[]{:S(2)}, u32[]{:S(2)}) collective-permute-start(bf16[128,6144]{1,0:T(8,128)(2,1)} %collective-permute-done.5), channel_id=1, source_target_pairs={{0,1},{1,2},{2,3},{3,4},{4,5},{5,6},{6,7},{7,8},{8,9},{9,10},{10,1... | collective-permute-start | bytes 4718600 | tf_op jit(solution)/shard_map/ppermute | solution.py:25
  246.6 35.1 %collective-permute-start.13 = (bf16[128,6144]{1,0:T(8,128)(2,1)}, bf16[128,6144]{1,0:T(8,128)(2,1)S(1)}, u32[]{:S(2)}, u32[]{:S(2)}) collective-permute-start(bf16[128,6144]{1,0:T(8,128)(2,1)} %collective-permute-done.12), channel_id=1, source_target_pairs={{1,0},{2,1},{3,2},{4,3},{5,4},{6,5},{7,6},{8,7},{9,8},{10,9},{11,1... | collective-permute-start | bytes 4718600 | tf_op jit(solution)/shard_map/ppermute | solution.py:27
  246.7 39.5 %collective-permute-start.7 = (bf16[128,6144]{1,0:T(8,128)(2,1)}, bf16[128,6144]{1,0:T(8,128)(2,1)S(1)}, u32[]{:S(2)}, u32[]{:S(2)}) collective-permute-start(bf16[128,6144]{1,0:T(8,128)(2,1)} %collective-permute-done.6), channel_id=1, source_target_pairs={{0,1},{1,2},{2,3},{3,4},{4,5},{5,6},{6,7},{7,8},{8,9},{9,10},{10,1... | collective-permute-start | bytes 4718600 | tf_op jit(solution)/shard_map/ppermute | solution.py:25
  248.5 44.7 %copy-start.74 = (f32[128]{0:T(128)}, f32[128]{0:T(128)S(1)}, u32[]{:S(2)}) copy-start(f32[128]{0:T(128)S(1)} %fusion.29) | copy-start | bytes 1540
  248.5 87.9 %copy-start.56 = (f32[128]{0:T(128)}, f32[128]{0:T(128)S(1)}, u32[]{:S(2)}) copy-start(f32[128]{0:T(128)S(1)} %fusion.69) | copy-start | bytes 1540
  248.7 105.6 %copy-start.42 = (f32[128,64]{0,1:T(8,128)}, f32[128,64]{0,1:T(8,128)S(1)}, u32[]{:S(2)}) copy-start(f32[128,64]{0,1:T(8,128)S(1)} %get-tuple-element.47) | copy-start | bytes 98308
  248.7 105.6 %copy-start.44 = (f32[128,64]{0,1:T(8,128)}, f32[128,64]{0,1:T(8,128)S(1)}, u32[]{:S(2)}) copy-start(f32[128,64]{0,1:T(8,128)S(1)} %get-tuple-element.48) | copy-start | bytes 98308
  248.9 87.5 %copy-start.39 = (f32[2048,1]{0,1:T(1,128)}, f32[2048,1]{0,1:T(1,128)S(1)}, u32[]{:S(2)}) copy-start(f32[2048,1]{0,1:T(1,128)S(1)} %get-tuple-element.46) | copy-start | bytes 24580
  248.9 98.8 %copy-start.46 = (f32[2048,1]{0,1:T(1,128)}, f32[2048,1]{0,1:T(1,128)S(1)}, u32[]{:S(2)}) copy-start(f32[2048,1]{0,1:T(1,128)S(1)} %get-tuple-element.44) | copy-start | bytes 24580
  248.9 98.8 %copy-start.48 = (f32[2048,1]{0,1:T(1,128)}, f32[2048,1]{0,1:T(1,128)S(1)}, u32[]{:S(2)}) copy-start(f32[2048,1]{0,1:T(1,128)S(1)} %get-tuple-element.45) | copy-start | bytes 24580
  248.9 162.0 %copy-start.50 = (f32[2048,1]{0,1:T(1,128)}, f32[2048,1]{0,1:T(1,128)S(1)}, u32[]{:S(2)}) copy-start(f32[2048,1]{0,1:T(1,128)S(1)} %get-tuple-element.43) | copy-start | bytes 24580
  248.9 44.3 %copy-start.38 = (bf16[128,6144]{1,0:T(8,128)(2,1)S(1)}, bf16[128,6144]{1,0:T(8,128)(2,1)}, u32[]{:S(2)}) copy-start(bf16[128,6144]{1,0:T(8,128)(2,1)} %copy-done.37) | copy-start | bytes 4718596
  281.7 35.1 %collective-permute-start.14 = (bf16[128,6144]{1,0:T(8,128)(2,1)S(1)}, bf16[128,6144]{1,0:T(8,128)(2,1)S(1)}, u32[]{:S(2)}, u32[]{:S(2)}) collective-permute-start(bf16[128,6144]{1,0:T(8,128)(2,1)S(1)} %collective-permute-done.13), channel_id=1, source_target_pairs={{1,0},{2,1},{3,2},{4,3},{5,4},{6,5},{7,6},{8,7},{9,8},{10,9},{11,1... | collective-permute-start | bytes 4718600 | tf_op jit(solution)/shard_map/ppermute | solution.py:27
  346.7 26.4 %copy-start = (f32[128,6144]{1,0:T(8,128)}, f32[128,6144]{1,0:T(8,128)S(1)}, u32[]{:S(2)}) copy-start(f32[128,6144]{1,0:T(8,128)S(1)} %fusion.47) | copy-start | bytes 9437188
  356.9 30.6 %copy-start.61 = (s32[256]{0:T(256)S(1)}, s32[256]{0:T(256)}, u32[]{:S(2)}) copy-start(s32[256]{0:T(256)} %copy-done.60) | copy-start | bytes 3076
  357.7 10.9 all-to-all-start.2
  368.6 10.9 all-to-all-start.1
  379.5 12.2 all-to-all-start
  394.1 11.8 copy-start.8
  395.8 10.1 all-to-all-start.3
  419.1 34.5 %copy-start.20 = (bf16[1,128,2048]{2,1,0:T(8,128)(2,1)S(1)}, bf16[1,128,2048]{2,1,0:T(8,128)(2,1)}, u32[]{:S(2)}) copy-start(bf16[1,128,2048]{2,1,0:T(8,128)(2,1)} %param.23) | copy-start | bytes 1572868
  419.1 148.5 %all-to-all-start.4 = ((bf16[16,96,2048]{2,1,0:T(8,128)(2,1)}), bf16[16,96,2048]{2,1,0:T(8,128)(2,1)}, u32[]{:S(2)}, u32[]{:S(2)}) async-start(bf16[16,96,2048]{2,1,0:T(8,128)(2,1)} %bitcast.234), calls=%async_computation.4 | async-start | bytes 12582912 | tf_op jit(solution)/shard_map/all_to_all | solution.py:191
  567.7 142.4 %all-to-all-start.6 = ((bf16[16,96,2048]{2,1,0:T(8,128)(2,1)}), bf16[16,96,2048]{2,1,0:T(8,128)(2,1)}, u32[]{:S(2)}, u32[]{:S(2)}) async-start(bf16[16,96,2048]{2,1,0:T(8,128)(2,1)} %multiply_convert_fusion), calls=%async_computation.6 | async-start | bytes 12582912 | tf_op jit(solution)/shard_map/all_to_all | solution.py:225
  596.0 11.8 copy-start.77
  710.0 18.2 %copy-start.76 = (bf16[1,2048,1024]{2,1,0:T(8,128)(2,1)S(1)}, bf16[1,2048,1024]{2,1,0:T(8,128)(2,1)}, u32[]{:S(2)}) copy-start(bf16[1,2048,1024]{2,1,0:T(8,128)(2,1)} %param.20) | copy-start | bytes 12582916
  728.2 12.2 copy-start.78
  728.2 12.2 copy-start.81
  752.1 142.2 %all-to-all-start.7 = ((bf16[16,96,2048]{2,1,0:T(8,128)(2,1)}), bf16[16,96,2048]{2,1,0:T(8,128)(2,1)}, u32[]{:S(2)}, u32[]{:S(2)}) async-start(bf16[16,96,2048]{2,1,0:T(8,128)(2,1)} %bitcast.238), calls=%async_computation.7 | async-start | bytes 12582912 | tf_op jit(solution)/shard_map/all_to_all | solution.py:245
  894.3 142.2 %all-to-all-start.5 = ((bf16[16,96,2048]{2,1,0:T(8,128)(2,1)}), bf16[16,96,2048]{2,1,0:T(8,128)(2,1)}, u32[]{:S(2)}, u32[]{:S(2)}) async-start(bf16[16,96,2048]{2,1,0:T(8,128)(2,1)} %bitcast.237), calls=%async_computation.5 | async-start | bytes 12582912 | tf_op jit(solution)/shard_map/all_to_all | solution.py:198
  922.4 281.6 %reduce-scatter.11.cloned.1.call-start = ((), (), s32[]{:S(2)}) async-start(), calls=%async_computation.20 | async-start | bytes 8912896 | tf_op jit(solution)/shard_map/reduce_scatter | solution.py:324
  1062.5 10.7 copy-start.53
  1062.5 10.7 copy-start.55
  1068.8 14.1 copy-start.3
  1068.8 14.1 copy-start.25
  1069.6 12.9 all-to-all-start.8
  1090.8 12.8 all-to-all-start.10
  1103.6 11.4 all-to-all-start.9
  1107.4 12.0 copy-start.43
  1107.4 12.0 copy-start.45
  1115.0 14.2 all-to-all-start.11
  1119.2 316.7 %reduce-scatter.9.cloned.1.call-start = ((), (), s32[]{:S(2)}) async-start(), calls=%async_computation.19 | async-start | bytes 26738688 | tf_op jit(solution)/shard_map/reduce_scatter | solution.py:321
  1148.4 343.7 %reduce-scatter.15.cloned.1.call-start = ((), (), s32[]{:S(2)}) async-start(), calls=%async_computation.22 | async-start | bytes 6291456 | tf_op jit(solution)/shard_map/reduce_scatter | solution.py:262
  1161.6 387.6 %reduce-scatter.13.cloned.1.call-start = ((), (), s32[]{:S(2)}) async-start(), calls=%async_computation.21 | async-start | bytes 6291456 | tf_op jit(solution)/shard_map/reduce_scatter | solution.py:259
  1174.6 431.2 %reduce-scatter.17.cloned.1.call-start = ((), (), s32[]{:S(2)}) async-start(), calls=%async_computation.23 | async-start | bytes 6291456 | tf_op jit(solution)/shard_map/reduce_scatter | solution.py:265
  1187.8 478.4 %reduce-scatter.19.cloned.1.call-start = ((), (), s32[]{:S(2)}) async-start(), calls=%async_computation.24 | async-start | bytes 557056
  1203.9 526.7 %all-reduce.9.cloned.1.call-start = ((), (), s32[]{:S(2)}) async-start(), calls=%async_computation.25 | async-start | bytes 4194304 | tf_op jit(solution)/shard_map/psum | solution.py:332
  1553.3 56.6 %copy-start.75 = (f32[128]{0:T(128)S(1)}, f32[128]{0:T(128)}, u32[]{:S(2)}) copy-start(f32[128]{0:T(128)} %copy-done.74) | copy-start | bytes 1540
  1553.3 56.6 %copy-start.5 = (f32[128,2048]{1,0:T(8,128)S(1)}, f32[128,2048]{1,0:T(8,128)}, u32[]{:S(2)}) copy-start(f32[128,2048]{1,0:T(8,128)} %copy-done.4) | copy-start | bytes 3145732
  (54 other events, 247.2 us)
Sparse Core Ops, SparseCore 0:
  207.5 107.4 all-gather.1
  1062.6 125.9 reduce-scatter.10
  1192.7 243.2 reduce-scatter.8
  1438.6 53.4 reduce-scatter.14
  1494.8 54.3 reduce-scatter.12
  1551.4 54.3 reduce-scatter.16
  1609.9 56.2 reduce-scatter.18
  1668.5 61.9 all-reduce.8
